TPU v7x, 256 devices: a whole 4x4x8 slice. The times are simulated.
256 devices in a mesh: freq: 32 (over z, x), brow: 2 (over y_hi), bcol: 4 (over y_lo, core).
Axes of the slice: x: 4, y: 4 (y_hi: 2, y_lo: 2; y = y_hi * 2 + y_lo), z: 8, core: 2. Of those that a mesh axis runs over, the one named last changes fastest.
Arguments:
- voltages: bfloat16 [2, 1024, 94208], P(None, ('brow', 'bcol', 'freq')), may hold values from -6 to 6
- fir_taps: float32 [16, 4096], replicated, may hold values from -1.5 to 1.5
Outputs:
- visibilities: float32 [2, 128, 1024, 2, 4, 128], P(None, 'freq', 'brow', None, 'bcol')
All inputs are finite; a program needn't handle non-finite values.
Results may differ from a plain program's by a relative error of at most 0.0036.
Values may be sent and summed in bfloat16 or wider, within the bound.
A program may use at most 64 MiB of HBM per device.

v0:
```python
import math
import jax
import jax.numpy as jnp
from jax import lax
from jax.sharding import PartitionSpec as P

CHANNELS = 4096
RADIX = 64
TAPS = 16
AVG = 32
FRAMES = 8


def dft_table(length):
    index = jnp.arange(length, dtype=jnp.int32)
    phase = index[:, None] * index[None, :] % length
    angle = phase.astype(jnp.float32) * (2.0 * math.pi / length)
    cosine = jnp.cos(angle)
    sine = jnp.sin(angle)
    return jnp.stack([jnp.stack([cosine, sine]), jnp.stack([-sine, cosine])])


def channelize(voltages, fir_taps, first, count):
    width = voltages.shape[1]
    frames = voltages.reshape(2, width, FRAMES + TAPS - 1, CHANNELS)

    def add_tap(tap, filtered):
        window = lax.dynamic_slice_in_dim(frames, first + tap, count, 2).astype(jnp.float32)
        return filtered + fir_taps[tap] * window

    filtered = lax.fori_loop(0, TAPS, add_tap, jnp.zeros((2, width, count, CHANNELS), jnp.float32))
    stacked = filtered.reshape(2, width, count, RADIX, RADIX)
    table = dft_table(RADIX)
    section = jnp.einsum("cwtbn,dcbk->dwtkn", stacked, table, precision=lax.Precision.HIGHEST)
    index = jnp.arange(RADIX, dtype=jnp.int32)
    phase = (index[:, None] * index[None, :]).astype(jnp.float32) * (2.0 * math.pi / CHANNELS)
    tw_cos = jnp.cos(phase)
    tw_sin = jnp.sin(phase)
    turned = jnp.stack(
        [section[0] * tw_cos + section[1] * tw_sin, section[1] * tw_cos - section[0] * tw_sin]
    )
    spectrum = jnp.einsum("cwtkn,dcnm->dwtmk", turned, table, precision=lax.Precision.HIGHEST) * (
        1.0 / RADIX
    )
    return spectrum.astype(jnp.bfloat16).reshape(2, width, count, CHANNELS)


def shards(voltages, fir_taps):
    local = channelize(voltages, fir_taps, 0, FRAMES)
    owned = lax.all_to_all(local, "freq", split_axis=3, concat_axis=1, tiled=True)
    group = owned.shape[3]
    coarse = group // AVG
    scale = 1.0 / (FRAMES * AVG)
    block = owned.shape[1]
    row_count = lax.axis_size("brow")
    col_block = lax.all_gather(owned, "brow", axis=1, tiled=True)
    left_rows = lax.all_gather(owned, "bcol", axis=1, tiled=True)
    left = left_rows.reshape(2, left_rows.shape[1], FRAMES, coarse, AVG)
    right = col_block.reshape(2, col_block.shape[1], FRAMES, coarse, AVG)
    flipped = jnp.stack([-right[1], right[0]])
    real_part = jnp.einsum("cptqa,cutqa->qpu", left, right, preferred_element_type=jnp.float32)
    imag_part = jnp.einsum("cptqa,cutqa->qpu", left, flipped, preferred_element_type=jnp.float32)
    result = jnp.stack([real_part, imag_part]) * scale
    return result.reshape(2, coarse, result.shape[2], row_count, 1, block)


def solution(mesh):
    in_specs = (P(None, ("brow", "bcol", "freq"), None), P())
    out_specs = P(None, "freq", "brow", None, "bcol", None)
    return jax.shard_map(shards, mesh=mesh, in_specs=in_specs, out_specs=out_specs, check_vma=False)
```

profile of v0, /device:TPU:1, one launch (start us, length us, event | category | flops | bytes accessed | tf_op | source)
XLA Modules:
  0.0 201.7 jit_solution(7456410314755574739)
XLA Ops:
  7.0 2.1 %reshape.165 = bf16[2,4,23,4096]{3,2,1,0:T(8,128)(2,1)S(1)} reshape(bf16[2,4,94208]{2,1,0:T(4,128)(2,1)} %param.4) | data formatting | bytes 3014656 | tf_op jit(solution)/shard_map/reshape | solution.py:25
  9.1 23.2 %while.14 = (s32[]{:T(128)}, f32[2,4,8,4096]{3,2,1,0:T(8,128)S(1)}, f32[16,4096]{1,0:T(8,128)}, bf16[2,4,23,4096]{3,2,1,0:T(8,128)(2,1)S(1)}, s32[]{:T(128)}, /*index=5*/s32[]{:T(128)}) while((s32[]{:T(128)}, f32[2,4,8,4096]{3,2,1,0:T(8,128)S(1)}, f32[16,4096]{1,0:T(8,128)}, bf16[2,4,23,4096]{3,2,1,0:T(8,128)(2,1)S(1)}, s32[]{:T(128)}, ...), condition=%wide.region_1.0_spmd.clone, body=%wide.region_0.0_spmd.clone.sunk | while | flops 1048579 | bytes 2670687 | solution.py:31
  9.1 0.9 constant_dynamic-slice_fusion.2
  10.1 0.5 select_add_fusion.2
  10.6 0.9 constant_dynamic-slice_fusion.2
  11.5 0.5 select_add_fusion.2
  12.0 0.9 constant_dynamic-slice_fusion.2
  13.5 0.9 constant_dynamic-slice_fusion.2
  14.9 0.9 constant_dynamic-slice_fusion.2
  15.8 0.5 select_add_fusion.2
  16.4 0.9 constant_dynamic-slice_fusion.2
  17.3 0.5 select_add_fusion.2
  17.8 0.9 constant_dynamic-slice_fusion.2
  18.7 0.5 select_add_fusion.2
  19.3 0.9 constant_dynamic-slice_fusion.2
  20.2 0.5 select_add_fusion.2
  20.7 0.9 constant_dynamic-slice_fusion.2
  21.6 0.5 select_add_fusion.2
  22.2 0.9 constant_dynamic-slice_fusion.2
  23.1 0.5 select_add_fusion.2
  23.6 0.9 constant_dynamic-slice_fusion.2
  24.5 0.5 select_add_fusion.2
  25.1 0.9 constant_dynamic-slice_fusion.2
  26.5 0.9 constant_dynamic-slice_fusion.2
  28.0 0.9 constant_dynamic-slice_fusion.2
  29.4 0.9 constant_dynamic-slice_fusion.2
  30.9 0.9 constant_dynamic-slice_fusion.2
  32.3 0.8 reshape.166
  33.2 2.0 fusion.7
  35.6 3.1 %fusion.12 = bf16[2,4,8,64,64]{4,3,2,1,0:T(8,128)(2,1)S(1)} fusion(f32[1,2,64,64]{2,3,1,0:T(8,128)S(1)} %get-tuple-element.113, f32[1,2,64,64]{2,3,1,0:T(8,128)S(1)} %get-tuple-element.112, f32[1,4,8,64,64]{4,3,2,1,0:T(8,128)S(1)} %get-tuple-element.109, f32[1,4,8,64,64]{4,3,2,1,0:T(8,128)S(1)} %get-tuple-element.108), kind=kOutput, calls=%fused_computation.13 | convolution fusion | flops 403456000 | bytes 1638400 | tf_op jit(solution)/shard_map/cwtkn,dcnm->dwtmk/dot_general | solution.py:42
  38.7 9.3 %copy.45 = bf16[2,4,8,64,64]{2,1,0,4,3:T(4,128)(2,1)} copy(bf16[2,4,8,64,64]{4,3,2,1,0:T(8,128)(2,1)S(1)} %fusion.12) | data formatting | bytes 1048576 | tf_op jit(solution)/shard_map/reshape | solution.py:45
  48.0 10.5 %reshape.177 = bf16[32,2,4096]{2,1,0:T(2,128)(2,1)S(1)} reshape(bf16[4096,2,4,8]{3,2,1,0:T(4,128)(2,1)} %bitcast.66) | data formatting | bytes 1048576
  58.5 27.9 %all_to_all.18 = bf16[32,2,4096]{2,1,0:T(2,128)(2,1)S(1)} all-to-all(bf16[32,2,4096]{2,1,0:T(2,128)(2,1)S(1)} %reshape.177), channel_id=1, replica_groups=mesh['freq'=32,'brow'=2,'bcol'=4] {'freq'}, dimensions={0} | all-to-all | bytes 1048576 | tf_op jit(solution)/shard_map/all_to_all | solution.py:50
  86.4 10.9 %reshape.178 = bf16[4096,2,4,8]{3,2,1,0:T(4,128)(2,1)} reshape(bf16[32,2,4096]{2,1,0:T(2,128)(2,1)S(1)} %all_to_all.18) | data formatting | bytes 1048576
  97.3 10.6 %copy.47 = bf16[2,4,8,32,128]{4,2,1,3,0:T(8,128)(2,1)} copy(bf16[2,4,8,32,128]{2,1,0,4,3:T(4,128)(2,1)} %bitcast.67) | data formatting | bytes 1048576 | tf_op jit(solution)/shard_map/all_to_all | solution.py:50
  108.1 0.5 all-gather.3.cloned.1.call-update
  108.7 25.4 %all-gather.5.cloned.1.call-done = bf16[2,256,8,128]{3,2,1,0:T(8,128)(2,1)} async-done(((bf16[2,128,8,128]{3,2,1,0:T(8,128)(2,1)}), bf16[2,256,8,128]{3,2,1,0:T(8,128)(2,1)}) %all-gather.5.cloned.1.call-update) | async-done | bytes 1048592 | tf_op jit(solution)/shard_map/all_gather | solution.py:56
  134.1 1.4 slice_negate_fusion
  135.5 1.1 copy.36
  136.6 1.1 copy.37
  137.7 0.7 copy.35
  138.4 29.0 %all-gather.3.cloned.1.call-done = bf16[2,512,8,128]{3,2,1,0:T(8,128)(2,1)} async-done(((bf16[2,128,8,128]{3,2,1,0:T(8,128)(2,1)}), bf16[2,512,8,128]{3,2,1,0:T(8,128)(2,1)}) %all-gather.3.cloned.1.call-update) | async-done | bytes 2097168 | tf_op jit(solution)/shard_map/all_gather | solution.py:57
  167.4 3.0 %copy.34 = bf16[2,512,8,128]{1,3,2,0:T(8,128)(2,1)S(1)} copy(bf16[2,512,8,128]{3,2,1,0:T(8,128)(2,1)} %all-gather.3.cloned.1.call-done) | data formatting | bytes 4194304 | tf_op jit(solution)/shard_map/all_gather | solution.py:57
  170.4 2.1 %fusion.33 = f32[4,512,256,1,1]{1,2,0,4,3:T(8,128)} fusion(bf16[2,512,8,4,32]{1,4,3,2,0:T(8,128)(2,1)S(1)} %bitcast.68, bf16[2,256,8,4,32]{1,4,3,2,0:T(8,128)(2,1)S(1)} %bitcast.74), kind=kOutput, calls=%fused_computation.42 | convolution fusion | flops 536870912 | bytes 5242880 | tf_op jit(solution)/shard_map/cptqa,cutqa->qpu/dot_general | solution.py:61
  172.5 6.1 %copy.38 = f32[1,4,512,2,1,128]{5,4,3,2,1,0:T(1,128)} copy(f32[1,4,512,2,1,128]{2,5,3,1,4,0:T(8,128)} %bitcast.71) | data formatting | bytes 4194304 | tf_op jit(solution)/shard_map/stack | solution.py:63
  178.7 2.1 %fusion.15 = f32[4,512,256,1,1]{1,2,0,4,3:T(8,128)} fusion(bf16[2,512,8,4,32]{1,4,3,2,0:T(8,128)(2,1)S(1)} %bitcast.69, bf16[1,256,8,4,32]{1,4,3,2,0:T(8,128)(2,1)S(1)} %bitcast.76, bf16[1,256,8,4,32]{1,4,3,2,0:T(8,128)(2,1)S(1)} %bitcast.75), kind=kOutput, calls=%fused_computation.14 | convolution fusion | flops 537395200 | bytes 5242880 | tf_op jit(solution)/shard_map/cptqa,cutqa->qpu/dot_general | solution.py:62
  180.7 6.2 %copy.39 = f32[1,4,512,2,1,128]{5,4,3,2,1,0:T(1,128)} copy(f32[1,4,512,2,1,128]{2,5,3,1,4,0:T(8,128)} %bitcast.70) | data formatting | bytes 4194304 | tf_op jit(solution)/shard_map/stack | solution.py:63
  186.9 7.9 %maximum_multiply_fusion = f32[2,4,512,2,1,128]{5,4,3,2,1,0:T(1,128)} fusion(f32[1,4,512,2,1,128]{5,4,3,2,1,0:T(1,128)} %copy.39, f32[1,4,512,2,1,128]{5,4,3,2,1,0:T(1,128)S(1)} %copy-done), kind=kLoop, calls=%fused_computation.2 | loop fusion | flops 2097152 | bytes 8388608 | tf_op jit(solution)/shard_map/mul | solution.py:63
  (24 shorter events, 4.6 us)
Async XLA Ops:
  6.5 127.5 %all-gather.5.cloned.1.call-start = ((), (), s32[]{:S(2)}) async-start(), calls=%async_computation.2 | async-start | bytes 1572864 | tf_op jit(solution)/shard_map/all_gather | solution.py:56
  107.9 59.5 %all-gather.3.cloned.1.call-start = ((), (), s32[]{:S(2)}) async-start(), calls=%async_computation.1 | async-start | bytes 2621440 | tf_op jit(solution)/shard_map/all_gather | solution.py:57
  134.1 3.7 %copy-start.1 = (bf16[2,256,8,128]{3,2,1,0:T(8,128)(2,1)S(1)}, bf16[2,256,8,128]{3,2,1,0:T(8,128)(2,1)}, u32[]{:S(2)}) copy-start(bf16[2,256,8,128]{3,2,1,0:T(8,128)(2,1)} %all-gather.5.cloned.1.call-done) | copy-start | bytes 3145732
  172.5 6.2 %copy-start.2 = (bf16[1,256,8,128]{1,3,2,0:T(8,128)(2,1)S(1)}, bf16[1,256,8,128]{1,3,2,0:T(8,128)(2,1)}, u32[]{:S(2)}) copy-start(bf16[1,256,8,128]{1,3,2,0:T(8,128)(2,1)} %copy.36) | copy-start | bytes 1572868
  172.5 6.2 %copy-start.3 = (bf16[1,256,8,128]{1,3,2,0:T(8,128)(2,1)S(1)}, bf16[1,256,8,128]{1,3,2,0:T(8,128)(2,1)}, u32[]{:S(2)}) copy-start(bf16[1,256,8,128]{1,3,2,0:T(8,128)(2,1)} %copy.37) | copy-start | bytes 1572868
  180.7 6.2 %copy-start = (f32[1,4,512,2,1,128]{5,4,3,2,1,0:T(1,128)S(1)}, f32[1,4,512,2,1,128]{5,4,3,2,1,0:T(1,128)}, u32[]{:S(2)}) copy-start(f32[1,4,512,2,1,128]{5,4,3,2,1,0:T(1,128)} %copy.38) | copy-start | bytes 6291460
Sparse Core Ops, SparseCore 0:
  108.0 25.9 all-gather.4
  135.9 31.4 all-gather.2
where the time goes:
time: 203 us; the launch traced here: 202 us
  local copies, waits for them, and re-layouts  77.2 us (38%)
  waiting for transfers between devices  55 us (27%)
  blocking collectives  27.9 us (14%)
  other arithmetic  18.2 us (9%)
  between operations  13.5 us (7%)
  matrix products  9.25 us (5%)
    all_gather x1, waiting for transfers between devices, shards(): left_rows = lax.all_gather(owned, 'bcol', axis=1, tiled=True)  29 us
    all_to_all x1, blocking collectives, shards(): lax.all_to_all(local, 'freq', split_axis=3, concat_axis=1, tiled=True)  27.9 us
    all_gather x1, waiting for transfers between devices, shards(): col_block = lax.all_gather(owned, 'brow', axis=1, tiled=True)  25.4 us
    unnamed x10, local copies, waits for them, and re-layouts  21.4 us
    dynamic_slice x16, local copies, waits for them, and re-layouts, add_tap(): return filtered + fir_taps[tap] * window  14.8 us
    another operation x2, local copies, waits for them, and re-layouts, shards(): result = jnp.stack([real_part, imag_part]) * scale  12.3 us
    all_to_all x1, local copies, waits for them, and re-layouts, shards(): lax.all_to_all(local, 'freq', split_axis=3, concat_axis=1, tiled=True)  10.6 us
    reshape x1, local copies, waits for them, and re-layouts, channelize(): return spectrum.astype(jnp.bfloat16).reshape(2, width, count, CHANNELS)  9.33 us
  transfers between devices with their start and end apart: 2, of which 2 were waited for; matrix products, arithmetic and copies ran while one was open for 2% of the time, Pallas kernels for 0%

commit v1 on v0

--- a/solution.py
+++ b/solution.py
@@ -47,7 +47,10 @@
 
 def shards(voltages, fir_taps):
     local = channelize(voltages, fir_taps, 0, FRAMES)
-    owned = lax.all_to_all(local, "freq", split_axis=3, concat_axis=1, tiled=True)
+    owned = jnp.concatenate(
+        lax.all_to_all(jnp.stack(jnp.split(local, lax.axis_size("freq"), axis=3)), "freq", 0, 0),
+        axis=1,
+    )
     group = owned.shape[3]
     coarse = group // AVG
     scale = 1.0 / (FRAMES * AVG)

time: 203 us -> 163 us (0.80)
  local copies, waits for them, and re-layouts: 77.2 us -> 38 us
    unnamed x10 -> x39, local copies, waits for them, and re-layouts: 21.4 us -> 0.43 us
    all_to_all x1, local copies, waits for them, and re-layouts: 10.6 us -> 0.83 us  [shards(): lax.all_to_all(jnp.stack(jnp.split(local, lax.axis_size('freq'), axis=3))...]
    reshape x1, local copies, waits for them, and re-layouts: 9.33 us -> 0.81 us  [channelize(): return spectrum.astype(jnp.bfloat16).reshape(2, width, count, CHANNELS)]
  transfers between devices with their start and end apart: 2 -> 2, of which waited for: 2 -> 2; matrix products, arithmetic and copies ran while one was open for 2% -> 3% of each run, Pallas kernels for 0% -> 0%
where the time goes in v1:
time: 163 us
  waiting for transfers between devices  55 us (34%)
  local copies, waits for them, and re-layouts  38 us (23%)
  blocking collectives  27.9 us (17%)
  other arithmetic  18.2 us (11%)
  between operations  13.7 us (8%)
  matrix products  9.25 us (6%)
    all_gather x1, waiting for transfers between devices, shards(): left_rows = lax.all_gather(owned, 'bcol', axis=1, tiled=True)  29 us
    all_to_all x1, blocking collectives, shards(): lax.all_to_all(jnp.stack(jnp.split(local, lax.axis_size('freq'), axis=3))...  27.9 us
    all_gather x1, waiting for transfers between devices, shards(): col_block = lax.all_gather(owned, 'brow', axis=1, tiled=True)  25.4 us
    dynamic_slice x16, local copies, waits for them, and re-layouts, add_tap(): return filtered + fir_taps[tap] * window  14.8 us
    another operation x2, local copies, waits for them, and re-layouts, shards(): result = jnp.stack([real_part, imag_part]) * scale  12.3 us
    add x16, other arithmetic, add_tap(): return filtered + fir_taps[tap] * window  8.05 us
    mul x1, other arithmetic, shards(): result = jnp.stack([real_part, imag_part]) * scale  7.92 us
  transfers between devices with their start and end apart: 2, of which 2 were waited for; matrix products, arithmetic and copies ran while one was open for 3% of the time, Pallas kernels for 0%

profile of v1, /device:TPU:1, one launch (start us, length us, event | category | flops | bytes accessed | tf_op | source)
XLA Modules:
  0.0 162.6 jit_solution(13767817322749985334)
XLA Ops:
  7.0 2.1 %reshape.171 = bf16[2,4,23,4096]{3,2,1,0:T(8,128)(2,1)S(1)} reshape(bf16[2,4,94208]{2,1,0:T(4,128)(2,1)} %param.4) | data formatting | bytes 3014656 | tf_op jit(solution)/shard_map/reshape | solution.py:25
  9.1 23.2 %while.14 = (s32[]{:T(128)}, f32[2,4,8,4096]{3,2,1,0:T(8,128)S(1)}, f32[16,4096]{1,0:T(8,128)}, bf16[2,4,23,4096]{3,2,1,0:T(8,128)(2,1)S(1)}, s32[]{:T(128)}, /*index=5*/s32[]{:T(128)}) while((s32[]{:T(128)}, f32[2,4,8,4096]{3,2,1,0:T(8,128)S(1)}, f32[16,4096]{1,0:T(8,128)}, bf16[2,4,23,4096]{3,2,1,0:T(8,128)(2,1)S(1)}, s32[]{:T(128)}, ...), condition=%wide.region_1.0_spmd.clone, body=%wide.region_0.0_spmd.clone.sunk | while | flops 1048579 | bytes 2670687 | solution.py:31
  9.1 0.9 constant_dynamic-slice_fusion.2
  10.1 0.5 select_add_fusion.2
  10.6 0.9 constant_dynamic-slice_fusion.2
  11.5 0.5 select_add_fusion.2
  12.0 0.9 constant_dynamic-slice_fusion.2
  13.5 0.9 constant_dynamic-slice_fusion.2
  14.9 0.9 constant_dynamic-slice_fusion.2
  15.8 0.5 select_add_fusion.2
  16.4 0.9 constant_dynamic-slice_fusion.2
  17.3 0.5 select_add_fusion.2
  17.8 0.9 constant_dynamic-slice_fusion.2
  18.7 0.5 select_add_fusion.2
  19.3 0.9 constant_dynamic-slice_fusion.2
  20.2 0.5 select_add_fusion.2
  20.7 0.9 constant_dynamic-slice_fusion.2
  21.6 0.5 select_add_fusion.2
  22.2 0.9 constant_dynamic-slice_fusion.2
  23.1 0.5 select_add_fusion.2
  23.6 0.9 constant_dynamic-slice_fusion.2
  24.5 0.5 select_add_fusion.2
  25.1 0.9 constant_dynamic-slice_fusion.2
  26.0 0.5 select_add_fusion.2
  26.5 0.9 constant_dynamic-slice_fusion.2
  27.4 0.5 select_add_fusion.2
  28.0 0.9 constant_dynamic-slice_fusion.2
  29.4 0.9 constant_dynamic-slice_fusion.2
  30.9 0.9 constant_dynamic-slice_fusion.2
  32.3 0.8 reshape.172
  33.2 2.0 %fusion.7 = f32[2,4,8,64,64]{4,3,2,1,0:T(8,128)S(1)} fusion(f32[2,4,8,64,64]{4,3,2,1,0:T(8,128)S(1)} %reshape.172, f32[1,2,64,64]{2,3,1,0:T(8,128)S(1)} %get-tuple-element.113, f32[1,2,64,64]{2,3,1,0:T(8,128)S(1)} %get-tuple-element.112), kind=kOutput, calls=%fused_computation.12 | convolution fusion | flops 402669568 | bytes 2162688 | tf_op jit(solution)/shard_map/cwtbn,dcbk->dwtkn/dot_general | solution.py:34
  35.6 3.1 %fusion.12 = bf16[2,4,8,64,64]{4,3,2,1,0:T(8,128)(2,1)S(1)} fusion(f32[1,2,64,64]{2,3,1,0:T(8,128)S(1)} %get-tuple-element.113, f32[1,2,64,64]{2,3,1,0:T(8,128)S(1)} %get-tuple-element.112, f32[1,4,8,64,64]{4,3,2,1,0:T(8,128)S(1)} %get-tuple-element.109, f32[1,4,8,64,64]{4,3,2,1,0:T(8,128)S(1)} %get-tuple-element.108), kind=kOutput, calls=%fused_computation.13 | convolution fusion | flops 403456000 | bytes 1638400 | tf_op jit(solution)/shard_map/cwtkn,dcnm->dwtmk/dot_general | solution.py:42
  38.7 0.8 reshape.173
  40.1 27.9 %all_to_all.5 = bf16[32,2,4,8,128]{4,3,2,1,0:T(8,128)(2,1)S(1)} all-to-all(bf16[32,2,4,8,128]{4,3,2,1,0:T(8,128)(2,1)S(1)} %constant_dynamic-update-slice_fusion), channel_id=1, replica_groups=mesh['freq'=32,'brow'=2,'bcol'=4] {'freq'}, dimensions={0} | all-to-all | bytes 1048576 | tf_op jit(solution)/shard_map/all_to_all | solution.py:51
  68.0 0.8 copy.53
  69.1 0.5 all-gather.3.cloned.1.call-update
  69.6 25.4 %all-gather.5.cloned.1.call-done = bf16[2,256,8,128]{3,2,1,0:T(8,128)(2,1)} async-done(((bf16[2,128,8,128]{3,2,1,0:T(8,128)(2,1)}), bf16[2,256,8,128]{3,2,1,0:T(8,128)(2,1)}) %all-gather.5.cloned.1.call-update) | async-done | bytes 1048592 | tf_op jit(solution)/shard_map/all_gather | solution.py:59
  95.0 1.4 slice_negate_fusion
  96.4 1.1 copy.56
  97.6 1.1 copy.57
  98.7 0.7 copy.55
  99.4 29.0 %all-gather.3.cloned.1.call-done = bf16[2,512,8,128]{3,2,1,0:T(8,128)(2,1)} async-done(((bf16[2,128,8,128]{3,2,1,0:T(8,128)(2,1)}), bf16[2,512,8,128]{3,2,1,0:T(8,128)(2,1)}) %all-gather.3.cloned.1.call-update) | async-done | bytes 2097168 | tf_op jit(solution)/shard_map/all_gather | solution.py:60
  128.4 3.0 %copy.54 = bf16[2,512,8,128]{1,3,2,0:T(8,128)(2,1)S(1)} copy(bf16[2,512,8,128]{3,2,1,0:T(8,128)(2,1)} %all-gather.3.cloned.1.call-done) | data formatting | bytes 4194304 | tf_op jit(solution)/shard_map/all_gather | solution.py:60
  131.4 2.1 %fusion.33 = f32[4,512,256,1,1]{1,2,0,4,3:T(8,128)} fusion(bf16[2,512,8,4,32]{1,4,3,2,0:T(8,128)(2,1)S(1)} %bitcast.191, bf16[2,256,8,4,32]{1,4,3,2,0:T(8,128)(2,1)S(1)} %bitcast.197), kind=kOutput, calls=%fused_computation.106 | convolution fusion | flops 536870912 | bytes 5242880 | tf_op jit(solution)/shard_map/cptqa,cutqa->qpu/dot_general | solution.py:64
  133.5 6.1 %copy.58 = f32[1,4,512,2,1,128]{5,4,3,2,1,0:T(1,128)} copy(f32[1,4,512,2,1,128]{2,5,3,1,4,0:T(8,128)} %bitcast.194) | data formatting | bytes 4194304 | tf_op jit(solution)/shard_map/stack | solution.py:66
  139.6 2.1 %fusion.15 = f32[4,512,256,1,1]{1,2,0,4,3:T(8,128)} fusion(bf16[2,512,8,4,32]{1,4,3,2,0:T(8,128)(2,1)S(1)} %bitcast.192, bf16[1,256,8,4,32]{1,4,3,2,0:T(8,128)(2,1)S(1)} %bitcast.199, bf16[1,256,8,4,32]{1,4,3,2,0:T(8,128)(2,1)S(1)} %bitcast.198), kind=kOutput, calls=%fused_computation.14 | convolution fusion | flops 537395200 | bytes 5242880 | tf_op jit(solution)/shard_map/cptqa,cutqa->qpu/dot_general | solution.py:65
  141.7 6.2 %copy.59 = f32[1,4,512,2,1,128]{5,4,3,2,1,0:T(1,128)} copy(f32[1,4,512,2,1,128]{2,5,3,1,4,0:T(8,128)} %bitcast.193) | data formatting | bytes 4194304 | tf_op jit(solution)/shard_map/stack | solution.py:66
  147.9 7.9 %maximum_multiply_fusion = f32[2,4,512,2,1,128]{5,4,3,2,1,0:T(1,128)} fusion(f32[1,4,512,2,1,128]{5,4,3,2,1,0:T(1,128)} %copy.59, f32[1,4,512,2,1,128]{5,4,3,2,1,0:T(1,128)S(1)} %copy-done), kind=kLoop, calls=%fused_computation.2 | loop fusion | flops 2097152 | bytes 8388608 | tf_op jit(solution)/shard_map/mul | solution.py:66
  (54 shorter events, 4.1 us)
Async XLA Ops:
  6.5 88.5 %all-gather.5.cloned.1.call-start = ((), (), s32[]{:S(2)}) async-start(), calls=%async_computation.2 | async-start | bytes 1572864 | tf_op jit(solution)/shard_map/all_gather | solution.py:59
  68.9 59.5 %all-gather.3.cloned.1.call-start = ((), (), s32[]{:S(2)}) async-start(), calls=%async_computation.1 | async-start | bytes 2621440 | tf_op jit(solution)/shard_map/all_gather | solution.py:60
  95.0 3.7 %copy-start.1 = (bf16[2,256,8,128]{3,2,1,0:T(8,128)(2,1)S(1)}, bf16[2,256,8,128]{3,2,1,0:T(8,128)(2,1)}, u32[]{:S(2)}) copy-start(bf16[2,256,8,128]{3,2,1,0:T(8,128)(2,1)} %all-gather.5.cloned.1.call-done) | copy-start | bytes 3145732
  133.5 6.2 %copy-start.2 = (bf16[1,256,8,128]{1,3,2,0:T(8,128)(2,1)S(1)}, bf16[1,256,8,128]{1,3,2,0:T(8,128)(2,1)}, u32[]{:S(2)}) copy-start(bf16[1,256,8,128]{1,3,2,0:T(8,128)(2,1)} %copy.56) | copy-start | bytes 1572868
  133.5 6.2 %copy-start.3 = (bf16[1,256,8,128]{1,3,2,0:T(8,128)(2,1)S(1)}, bf16[1,256,8,128]{1,3,2,0:T(8,128)(2,1)}, u32[]{:S(2)}) copy-start(bf16[1,256,8,128]{1,3,2,0:T(8,128)(2,1)} %copy.57) | copy-start | bytes 1572868
  141.7 6.2 %copy-start = (f32[1,4,512,2,1,128]{5,4,3,2,1,0:T(1,128)S(1)}, f32[1,4,512,2,1,128]{5,4,3,2,1,0:T(1,128)}, u32[]{:S(2)}) copy-start(f32[1,4,512,2,1,128]{5,4,3,2,1,0:T(1,128)} %copy.58) | copy-start | bytes 6291460
Sparse Core Ops, SparseCore 0:
  69.0 25.9 all-gather.4
  96.8 31.4 all-gather.2
